TPU v7x, 128 devices: a whole 4x4x4 slice. The times are simulated.
128 devices in a mesh: tm: 2 (over core), rows: 64 (over z, x, y).
Axes of the slice: x: 4, y: 4, z: 4, core: 2. Of those that a mesh axis runs over, the one named last changes fastest.
Arguments:
- feat: bfloat16 [4, 128, 240, 512], P('tm', 'rows'), may hold values from -24 to 24
- norm1_gain: float32 [512], replicated, may hold values from 0.5 to 1.5
- norm1_bias: float32 [512], replicated, may hold values from -3 to 3
- conv_weight: bfloat16 [3, 3, 3, 512, 512], replicated, may hold values from -0.0546875 to 0.0546875
- conv_bias: float32 [512], replicated, may hold values from -3 to 3
- norm2_gain: float32 [512], replicated, may hold values from 0.5 to 1.5
- norm2_bias: float32 [512], replicated, may hold values from -3 to 3
- w_query: bfloat16 [512, 512], replicated, may hold values from -0.44194174 to 0.44194174
- w_key: bfloat16 [512, 512], replicated, may hold values from -1.5467961 to 1.5467961
- w_value: bfloat16 [512, 512], replicated, may hold values from -0.25 to 0.25
- w_out: bfloat16 [512, 512], replicated, may hold values from -0.25 to 0.25
- out_bias: float32 [512], replicated, may hold values from -3 to 3
Outputs:
- block_out: bfloat16 [4, 128, 240, 512], P('tm', 'rows')
All inputs are finite; a program needn't handle non-finite values.
Results may differ from a plain program's by a relative error of at most 0.0062.
The roundings to bfloat16 on the way count: a program that leaves them out, or rounds other values in their place, can miss the bound.
Values may be sent and summed in bfloat16 or wider, within the bound.
No kernel may reach another device: no remote copies, remote signals or barrier semaphores. Data moves between devices by JAX's collectives and lax.ppermute only.
A program may use at most 128 MiB of HBM per device.

v0:
```python
import math
import jax
import jax.numpy as jnp
from jax import lax
from jax.sharding import PartitionSpec as P

GROUPS = 32
RADIUS = 4
EPS = 1e-06


def from_behind(array, axis, by):
    peers = lax.axis_size(axis)
    pairs = [(i, i + by) for i in range(peers) if 0 <= i + by < peers]
    return lax.ppermute(array, axis, pairs)


def padded_2(cells, sides, width):
    for axis, dim in sides:
        count = lax.axis_size(axis)
        ends = count - 1
        head = lax.slice_in_dim(cells, 0, width, axis=dim)
        tail = lax.slice_in_dim(cells, cells.shape[dim] - width, cells.shape[dim], axis=dim)
        cells = jnp.concatenate(
            [
                lax.ppermute(tail, axis, [(i, (i + 1) % count) for i in range(ends)]),
                cells,
                lax.ppermute(head, axis, [((i + 1) % count, i) for i in range(ends)]),
            ],
            axis=dim,
        )
    return cells


def group_norm(values, gain, shift, count):
    chans = values.shape[-1]
    grouped = values.reshape(values.shape[:-1] + (GROUPS, chans // GROUPS))
    local_sum = jnp.sum(grouped, axis=(0, 1, 2, 4))
    mean = lax.psum(local_sum, ("tm", "rows")) / count
    centered = grouped - mean[:, None]
    spread = lax.psum(jnp.sum(centered * centered, axis=(0, 1, 2, 4)), ("tm", "rows")) / count
    normed = centered * lax.rsqrt(spread + EPS)[:, None]
    return normed.reshape(values.shape) * gain + shift


def conv_taps(padded, weight, frames, height, width):
    chans = padded.shape[-1]
    total = jnp.zeros((frames * height * width, weight.shape[-1]), jnp.float32)
    for step_t in range(3):
        for step_h in range(3):
            slab = padded[step_t : step_t + frames, step_h : step_h + height]
            stacked = jnp.concatenate(
                [slab[:, :, step_w : step_w + width] for step_w in range(3)], axis=-1
            )
            total = total + jnp.dot(
                stacked.reshape(-1, 3 * chans),
                weight[step_t, step_h].reshape(3 * chans, -1),
                preferred_element_type=jnp.float32,
            )
    return total.reshape(frames, height, width, -1)


def project(flat, weight):
    return jnp.dot(flat, weight, preferred_element_type=jnp.float32).astype(jnp.bfloat16)


def shards(
    feat,
    norm1_gain,
    norm1_bias,
    conv_weight,
    conv_bias,
    norm2_gain,
    norm2_bias,
    w_query,
    w_key,
    w_value,
    w_out,
    out_bias,
):
    frames, stripe_rows, width, chans = feat.shape
    stripes = lax.axis_size("rows")
    count = lax.axis_size("tm") * stripes * frames * stripe_rows * width * (chans // GROUPS)
    act = jax.nn.silu(group_norm(feat.astype(jnp.float32), norm1_gain, norm1_bias, count)).astype(
        jnp.bfloat16
    )
    earlier = from_behind(act, "tm", 1)
    opening = jnp.broadcast_to(act[:1], earlier.shape)
    earlier = jnp.where(lax.axis_index("tm") == 0, opening, earlier)
    timed = jnp.concatenate([earlier, act], axis=0)
    rimmed = padded_2(timed, (("rows", 1),), 1)
    padded = jnp.pad(rimmed, ((0, 0), (0, 0), (1, 1), (0, 0)))
    conv = conv_taps(padded, conv_weight, frames, stripe_rows, width) + conv_bias
    resid = (feat.astype(jnp.float32) + conv).astype(jnp.bfloat16)
    normed = group_norm(resid.astype(jnp.float32), norm2_gain, norm2_bias, count).astype(
        jnp.bfloat16
    )
    flat = normed.reshape(-1, chans)
    query = project(flat, w_query).reshape(frames, -1, chans)
    reach = RADIUS * stripe_rows
    paired = jnp.stack([project(flat, w_key), project(flat, w_value)]).reshape(
        2, frames, stripe_rows, width, chans
    )
    pieces = []
    for offset in range(-RADIUS, RADIUS + 1):
        if offset == 0:
            pieces.append(paired)
        else:
            pieces.append(from_behind(paired, "rows", -offset))
    wide = jnp.concatenate(pieces, axis=2)
    keys = wide[0].reshape(frames, -1, chans)
    values = wide[1].reshape(frames, -1, chans)
    span = 2 * reach + stripe_rows
    place = lax.axis_index("rows") * stripe_rows - reach + jnp.arange(span, dtype=jnp.int32)
    valid = jnp.repeat((place >= 0) & (place < stripes * stripe_rows), width)
    scale = 1.0 / math.sqrt(chans)
    scores = jnp.einsum("fqc,fkc->fqk", query, keys, preferred_element_type=jnp.float32) * scale
    scores = jnp.where(valid[None, None, :], scores, jnp.float32(-1e30))
    top = jnp.max(scores, axis=-1, keepdims=True)
    expo = jnp.exp(scores - top)
    total = jnp.sum(expo, axis=-1, keepdims=True)
    mixed = jnp.einsum(
        "fqk,fkc->fqc", expo.astype(jnp.bfloat16), values, preferred_element_type=jnp.float32
    )
    attn = (mixed / total).astype(jnp.bfloat16).reshape(-1, chans)
    output = jnp.dot(attn, w_out, preferred_element_type=jnp.float32).reshape(
        frames, stripe_rows, width, chans
    )
    return (resid.astype(jnp.float32) + out_bias + output).astype(jnp.bfloat16)


def solution(mesh):
    return jax.shard_map(
        shards,
        mesh=mesh,
        in_specs=(
            P("tm", "rows", None, None),
            P(),
            P(),
            P(),
            P(),
            P(),
            P(),
            P(),
            P(),
            P(),
            P(),
            P(),
        ),
        out_specs=P("tm", "rows", None, None),
        check_vma=False,
    )
```

profile of v0, /device:TPU:54, one launch (start us, length us, event | category | flops | bytes accessed | tf_op | source)
XLA Modules:
  0.0 680.6 jit_solution(8682278299150185639)
XLA Ops:
  1.7 63.7 %psum.28 = f32[32]{0:T(128)S(1)} all-reduce(f32[32]{0:T(128)S(1)} %reduce_sum.59), channel_id=1, replica_groups=mesh['tm'=2,'rows'=64] {'tm','rows'}, use_global_device_ids=true, to_apply=%region_2.0 | all-reduce | flops 32 | bytes 256 | tf_op jit(solution)/shard_map/psum | solution.py:39
  67.2 63.0 %psum.29 = f32[32]{0:T(128)S(1)} all-reduce(f32[32]{0:T(128)S(1)} %reduce_sum.62), channel_id=1, replica_groups=mesh['tm'=2,'rows'=64] {'tm','rows'}, use_global_device_ids=true, to_apply=%region_5.6 | all-reduce | flops 32 | bytes 256 | tf_op jit(solution)/shard_map/psum | solution.py:41
  130.4 1.9 fusion.31
  132.3 1.7 collective-permute-start
  134.1 2.1 collective-permute-done
  136.5 3.7 collective-permute-start.1
  140.2 2.4 collective-permute-start.2
  142.5 9.3 %fusion.44 = (bf16[1,1,3,512,512]{4,3,2,1,0:T(8,128)(2,1)S(1)}, bf16[1,1,3,512,512]{4,3,2,1,0:T(8,128)(2,1)}, bf16[1,1,3,512,512]{4,3,2,1,0:T(8,128)(2,1)}, bf16...) fusion(bf16[3,3,3,512,512]{4,3,2,1,0:T(8,128)(2,1)} %param.15), kind=kLoop, calls=%fused_computation.89 | loop fusion | bytes 28311552 | tf_op jit(solution)/shard_map/slice | solution.py:57
  151.8 10.6 %collective-permute-done.1 = bf16[4,1,240,512]{3,2,1,0:T(8,128)(2,1)S(1)} collective-permute-done((bf16[4,1,240,512]{3,2,1,0:T(8,128)(2,1)S(1)}, bf16[4,1,240,512]{3,2,1,0:T(8,128)(2,1)S(1)}, u32[]{:S(2)}, u32[]{:S(2)}) %collective-permute-start.1) | collective-permute-done | bytes 983072 | tf_op jit(solution)/shard_map/ppermute | solution.py:26
  162.4 4.4 collective-permute-done.2
  166.8 2.1 select_maximum_fusion
  168.8 6.3 fusion.45
  179.5 1.7 fusion.48
  181.2 1.7 fusion.50
  184.7 1.7 fusion.51
  186.4 1.7 fusion.53
  189.5 1.7 fusion.54
  192.6 1.7 fusion.49
  194.3 1.7 fusion.52
  196.0 1.7 fusion.55
  197.7 2.5 add_add_fusion
  200.8 66.5 %psum.30 = f32[32]{0:T(128)S(1)} all-reduce(f32[32]{0:T(128)S(1)} %reduce_sum.81), channel_id=1, replica_groups=mesh['tm'=2,'rows'=64] {'tm','rows'}, use_global_device_ids=true, to_apply=%region_8.9 | all-reduce | flops 32 | bytes 256 | tf_op jit(solution)/shard_map/psum | solution.py:39
  268.0 64.1 %psum.31 = f32[32]{0:T(128)S(1)} all-reduce(f32[32]{0:T(128)S(1)} %reduce_sum.84), channel_id=1, replica_groups=mesh['tm'=2,'rows'=64] {'tm','rows'}, use_global_device_ids=true, to_apply=%region_11.12 | all-reduce | flops 32 | bytes 256 | tf_op jit(solution)/shard_map/psum | solution.py:41
  333.4 1.7 convolution_convert_fusion
  336.6 3.8 collective-permute-start.3
  340.4 3.2 collective-permute-start.4
  343.6 4.6 collective-permute-start.5
  348.2 3.0 collective-permute-start.6
  351.2 2.8 collective-permute-start.7
  354.1 30.5 %collective-permute-done.3 = bf16[2,2,2,240,512]{4,3,2,1,0:T(8,128)(2,1)} collective-permute-done((bf16[2,2,2,240,512]{4,3,2,1,0:T(8,128)(2,1)}, bf16[2,2,2,240,512]{4,3,2,1,0:T(8,128)(2,1)}, u32[]{:S(2)}, u32[]{:S(2)}) %collective-permute-start.3) | collective-permute-done | bytes 1966112 | tf_op jit(solution)/shard_map/ppermute | solution.py:15
  384.6 2.5 collective-permute-start.8
  387.1 39.4 %collective-permute-done.4 = bf16[2,2,2,240,512]{4,3,2,1,0:T(8,128)(2,1)} collective-permute-done((bf16[2,2,2,240,512]{4,3,2,1,0:T(8,128)(2,1)}, bf16[2,2,2,240,512]{4,3,2,1,0:T(8,128)(2,1)}, u32[]{:S(2)}, u32[]{:S(2)}) %collective-permute-start.4) | collective-permute-done | bytes 1966112 | tf_op jit(solution)/shard_map/ppermute | solution.py:15
  426.5 90.0 %collective-permute-start.9 = (bf16[2,2,2,240,512]{4,3,2,1,0:T(8,128)(2,1)}, bf16[2,2,2,240,512]{4,3,2,1,0:T(8,128)(2,1)}, u32[]{:S(2)}, u32[]{:S(2)}) collective-permute-start(bf16[2,2,2,240,512]{4,3,2,1,0:T(8,128)(2,1)} %pad_maximum_fusion.10), channel_id=1, source_target_pairs={{3,0},{4,1},{5,2},{6,3},{7,4},{8,5},{9,6},{10,7},{11,8},{12,9},{13... | collective-permute-start | bytes 5898248 | tf_op jit(solution)/shard_map/ppermute | solution.py:15
  516.5 3.1 collective-permute-start.10
  519.8 2.7 convolution_convert_fusion.2
  522.5 1.7 constant_dynamic-update-slice_fusion.8
  524.2 1.7 constant_dynamic-update-slice_fusion.7
  525.9 1.7 constant_dynamic-update-slice_fusion.6
  527.6 1.7 constant_dynamic-update-slice_fusion.5
  529.4 1.7 constant_dynamic-update-slice_fusion.3
  531.1 1.7 constant_dynamic-update-slice_fusion.2
  532.8 27.3 %collective-permute-done.9 = bf16[2,2,2,240,512]{4,3,2,1,0:T(8,128)(2,1)} collective-permute-done((bf16[2,2,2,240,512]{4,3,2,1,0:T(8,128)(2,1)}, bf16[2,2,2,240,512]{4,3,2,1,0:T(8,128)(2,1)}, u32[]{:S(2)}, u32[]{:S(2)}) %collective-permute-start.9) | collective-permute-done | bytes 1966112 | tf_op jit(solution)/shard_map/ppermute | solution.py:15
  561.7 80.5 %collective-permute-done.10 = bf16[2,2,2,240,512]{4,3,2,1,0:T(8,128)(2,1)} collective-permute-done((bf16[2,2,2,240,512]{4,3,2,1,0:T(8,128)(2,1)}, bf16[2,2,2,240,512]{4,3,2,1,0:T(8,128)(2,1)}, u32[]{:S(2)}, u32[]{:S(2)}) %collective-permute-start.10) | collective-permute-done | bytes 1966112 | tf_op jit(solution)/shard_map/ppermute | solution.py:15
  642.2 1.7 constant_dynamic-update-slice_fusion
  643.9 4.3 fusion.43
  648.2 10.2 %fusion = (f32[2,480]{1,0:T(2,128)S(1)}, f32[2,480,4320]{2,1,0:T(8,128)}) fusion(pred[4320]{0:T(1024)(128)(4,1)S(1)} %broadcast_in_dim.35, bf16[2,480,512]{2,1,0:T(8,128)(2,1)} %bitcast.89, bf16[2,4320,512]{2,1,0:T(8,128)(2,1)S(1)} %bitcast.63), kind=kOutput, calls=%fused_computation.2 | convolution fusion | flops 4259173376 | bytes 26427360 | tf_op jit(solution)/shard_map/fqc,fkc->fqk/dot_general | solution.py:117
  658.4 9.5 %fusion.1 = f32[2,480]{1,0:T(2,128)S(1)} fusion(f32[2,480,4320]{2,1,0:T(8,128)} %get-tuple-element.50, f32[2,480]{1,0:T(2,128)S(1)} %get-tuple-element.49, pred[4320]{0:T(1024)(128)(4,1)S(1)} %broadcast_in_dim.35), kind=kLoop, calls=%fused_computation.3 | loop fusion | flops 16587840 | bytes 16600800 | tf_op jit(solution)/shard_map/reduce_sum | solution.py:121
  667.9 11.0 %divide_convert_fusion = bf16[2,480,512]{2,1,0:T(8,128)(2,1)S(1)} fusion(bf16[2,4320,512]{2,1,0:T(8,128)(2,1)} %bitcast.62, f32[2,480,4320]{2,1,0:T(8,128)} %get-tuple-element.50, f32[2,480]{1,0:T(2,128)S(1)} %get-tuple-element.49, pred[4320]{0:T(1024)(128)(4,1)S(1)} %broadcast_in_dim.35, f32[2,480]{1,0:T(2,128)S(1)} %fusion.1), kind=kOutput, calls=%fused_computation.62 | convolution fusion | flops 4264304640 | bytes 26431200 | tf_op jit(solution)/shard_map/fqk,fkc->fqc/dot_general | solution.py:122
  (105 shorter events, 20.6 us)
Async XLA Ops:
  0.0 332.7 %copy-start = (bf16[512,512]{1,0:T(8,128)(2,1)S(1)}, bf16[512,512]{1,0:T(8,128)(2,1)}, u32[]{:S(2)}) copy-start(bf16[512,512]{1,0:T(8,128)(2,1)} %param.20) | copy-start | bytes 1572868
  132.3 3.9 collective-permute-start
  136.5 25.9 %collective-permute-start.1 = (bf16[4,1,240,512]{3,2,1,0:T(8,128)(2,1)S(1)}, bf16[4,1,240,512]{3,2,1,0:T(8,128)(2,1)S(1)}, u32[]{:S(2)}, u32[]{:S(2)}) collective-permute-start(bf16[4,1,240,512]{3,2,1,0:T(8,128)(2,1)S(1)} %get-tuple-element.44), channel_id=1, source_target_pairs={{0,1},{1,2},{2,3},{3,4},{4,5},{5,6},{6,7},{7,8},{8,9},{9,10},{10,1... | collective-permute-start | bytes 2949128 | tf_op jit(solution)/shard_map/ppermute | solution.py:26
  140.2 26.6 %collective-permute-start.2 = (bf16[4,1,240,512]{3,2,1,0:T(8,128)(2,1)S(1)}, bf16[4,1,240,512]{3,2,1,0:T(8,128)(2,1)S(1)}, u32[]{:S(2)}, u32[]{:S(2)}) collective-permute-start(bf16[4,1,240,512]{3,2,1,0:T(8,128)(2,1)S(1)} %get-tuple-element.45), channel_id=1, source_target_pairs={{1,0},{2,1},{3,2},{4,3},{5,4},{6,5},{7,6},{8,7},{9,8},{10,9},{11,1... | collective-permute-start | bytes 2949128 | tf_op jit(solution)/shard_map/ppermute | solution.py:28
  176.0 1.2 copy-start.10
  176.0 1.5 copy-start.11
  176.0 1.8 copy-start.12
  176.0 2.1 copy-start.13
  178.1 1.4 copy-start.21
  179.5 1.7 copy-start.20
  181.2 1.7 copy-start.6
  181.2 1.7 copy-start.7
  181.2 1.8 copy-start.8
  181.2 2.1 copy-start.9
  183.3 1.4 copy-start.19
  184.7 1.7 copy-start.18
  186.4 1.7 copy-start.5
  188.1 1.4 copy-start.17
  191.2 1.4 copy-start.16
  192.6 1.7 copy-start.15
  194.3 1.7 copy-start.14
  197.7 2.5 copy-start.2
  197.7 2.5 copy-start.24
  200.2 132.1 %copy-start.25 = (f32[512]{0:T(512)S(1)}, f32[512]{0:T(512)}, u32[]{:S(2)}) copy-start(f32[512]{0:T(512)} %param.18) | copy-start | bytes 6148
  200.2 132.1 %copy-start.26 = (f32[512]{0:T(512)S(1)}, f32[512]{0:T(512)}, u32[]{:S(2)}) copy-start(f32[512]{0:T(512)} %param.17) | copy-start | bytes 6148
  200.6 132.8 %copy-start.3 = (bf16[2,2,240,512]{3,2,1,0:T(8,128)(2,1)}, bf16[2,2,240,512]{3,2,1,0:T(8,128)(2,1)S(1)}, u32[]{:S(2)}) copy-start(bf16[2,2,240,512]{3,2,1,0:T(8,128)(2,1)S(1)} %get-tuple-element.6) | copy-start | bytes 2949124
  332.7 2.4 copy-start.22
  335.1 184.7 %copy-start.23 = (bf16[2,2,240,512]{3,2,1,0:T(8,128)(2,1)S(1)}, bf16[2,2,240,512]{3,2,1,0:T(8,128)(2,1)}, u32[]{:S(2)}) copy-start(bf16[2,2,240,512]{3,2,1,0:T(8,128)(2,1)} %copy-done.22) | copy-start | bytes 2949124
  336.6 48.0 %collective-permute-start.3 = (bf16[2,2,2,240,512]{4,3,2,1,0:T(8,128)(2,1)}, bf16[2,2,2,240,512]{4,3,2,1,0:T(8,128)(2,1)}, u32[]{:S(2)}, u32[]{:S(2)}) collective-permute-start(bf16[2,2,2,240,512]{4,3,2,1,0:T(8,128)(2,1)} %pad_maximum_fusion.10), channel_id=1, source_target_pairs={{0,4},{1,5},{2,6},{3,7},{4,8},{5,9},{6,10},{7,11},{8,12},{9,13},{1... | collective-permute-start | bytes 5898248 | tf_op jit(solution)/shard_map/ppermute | solution.py:15
  340.4 86.0 %collective-permute-start.4 = (bf16[2,2,2,240,512]{4,3,2,1,0:T(8,128)(2,1)}, bf16[2,2,2,240,512]{4,3,2,1,0:T(8,128)(2,1)}, u32[]{:S(2)}, u32[]{:S(2)}) collective-permute-start(bf16[2,2,2,240,512]{4,3,2,1,0:T(8,128)(2,1)} %pad_maximum_fusion.10), channel_id=1, source_target_pairs={{0,3},{1,4},{2,5},{3,6},{4,7},{5,8},{6,9},{7,10},{8,11},{9,12},{10... | collective-permute-start | bytes 5898248 | tf_op jit(solution)/shard_map/ppermute | solution.py:15
  343.6 172.8 %collective-permute-start.5 = (bf16[2,2,2,240,512]{4,3,2,1,0:T(8,128)(2,1)}, bf16[2,2,2,240,512]{4,3,2,1,0:T(8,128)(2,1)}, u32[]{:S(2)}, u32[]{:S(2)}) collective-permute-start(bf16[2,2,2,240,512]{4,3,2,1,0:T(8,128)(2,1)} %pad_maximum_fusion.10), channel_id=1, source_target_pairs={{0,2},{1,3},{2,4},{3,5},{4,6},{5,7},{6,8},{7,9},{8,10},{9,11},{10,... | collective-permute-start | bytes 5898248 | tf_op jit(solution)/shard_map/ppermute | solution.py:15
  348.2 179.4 %collective-permute-start.6 = (bf16[2,2,2,240,512]{4,3,2,1,0:T(8,128)(2,1)}, bf16[2,2,2,240,512]{4,3,2,1,0:T(8,128)(2,1)}, u32[]{:S(2)}, u32[]{:S(2)}) collective-permute-start(bf16[2,2,2,240,512]{4,3,2,1,0:T(8,128)(2,1)} %pad_maximum_fusion.10), channel_id=1, source_target_pairs={{0,1},{1,2},{2,3},{3,4},{4,5},{5,6},{6,7},{7,8},{8,9},{9,10},{10,1... | collective-permute-start | bytes 5898248 | tf_op jit(solution)/shard_map/ppermute | solution.py:15
  351.2 178.2 %collective-permute-start.7 = (bf16[2,2,2,240,512]{4,3,2,1,0:T(8,128)(2,1)}, bf16[2,2,2,240,512]{4,3,2,1,0:T(8,128)(2,1)}, u32[]{:S(2)}, u32[]{:S(2)}) collective-permute-start(bf16[2,2,2,240,512]{4,3,2,1,0:T(8,128)(2,1)} %pad_maximum_fusion.10), channel_id=1, source_target_pairs={{1,0},{2,1},{3,2},{4,3},{5,4},{6,5},{7,6},{8,7},{9,8},{10,9},{11,1... | collective-permute-start | bytes 5898248 | tf_op jit(solution)/shard_map/ppermute | solution.py:15
  384.6 146.5 %collective-permute-start.8 = (bf16[2,2,2,240,512]{4,3,2,1,0:T(8,128)(2,1)}, bf16[2,2,2,240,512]{4,3,2,1,0:T(8,128)(2,1)}, u32[]{:S(2)}, u32[]{:S(2)}) collective-permute-start(bf16[2,2,2,240,512]{4,3,2,1,0:T(8,128)(2,1)} %pad_maximum_fusion.10), channel_id=1, source_target_pairs={{2,0},{3,1},{4,2},{5,3},{6,4},{7,5},{8,6},{9,7},{10,8},{11,9},{12,... | collective-permute-start | bytes 5898248 | tf_op jit(solution)/shard_map/ppermute | solution.py:15
  426.5 133.6 %collective-permute-start.9 = (bf16[2,2,2,240,512]{4,3,2,1,0:T(8,128)(2,1)}, bf16[2,2,2,240,512]{4,3,2,1,0:T(8,128)(2,1)}, u32[]{:S(2)}, u32[]{:S(2)}) collective-permute-start(bf16[2,2,2,240,512]{4,3,2,1,0:T(8,128)(2,1)} %pad_maximum_fusion.10), channel_id=1, source_target_pairs={{3,0},{4,1},{5,2},{6,3},{7,4},{8,5},{9,6},{10,7},{11,8},{12,9},{13... | collective-permute-start | bytes 5898248 | tf_op jit(solution)/shard_map/ppermute | solution.py:15
  516.5 125.7 %collective-permute-start.10 = (bf16[2,2,2,240,512]{4,3,2,1,0:T(8,128)(2,1)}, bf16[2,2,2,240,512]{4,3,2,1,0:T(8,128)(2,1)}, u32[]{:S(2)}, u32[]{:S(2)}) collective-permute-start(bf16[2,2,2,240,512]{4,3,2,1,0:T(8,128)(2,1)} %pad_maximum_fusion.10), channel_id=1, source_target_pairs={{4,0},{5,1},{6,2},{7,3},{8,4},{9,5},{10,6},{11,7},{12,8},{13,9},{1... | collective-permute-start | bytes 5898248 | tf_op jit(solution)/shard_map/ppermute | solution.py:15
  667.9 11.1 %copy-start.4 = (bf16[2,2,240,512]{3,2,1,0:T(8,128)(2,1)S(1)}, bf16[2,2,240,512]{3,2,1,0:T(8,128)(2,1)}, u32[]{:S(2)}) copy-start(bf16[2,2,240,512]{3,2,1,0:T(8,128)(2,1)} %copy-done.3) | copy-start | bytes 2949124
  667.9 11.1 %copy-start.27 = (bf16[512,512]{1,0:T(8,128)(2,1)S(1)}, bf16[512,512]{1,0:T(8,128)(2,1)}, u32[]{:S(2)}) copy-start(bf16[512,512]{1,0:T(8,128)(2,1)} %param.22) | copy-start | bytes 1572868
  667.9 11.1 %copy-start.28 = (f32[512]{0:T(512)S(1)}, f32[512]{0:T(512)}, u32[]{:S(2)}) copy-start(f32[512]{0:T(512)} %param.23) | copy-start | bytes 6148
  667.9 12.7 %copy-start.1 = (bf16[512,512]{1,0:T(8,128)(2,1)S(1)}, bf16[512,512]{1,0:T(8,128)(2,1)}, u32[]{:S(2)}) copy-start(bf16[512,512]{1,0:T(8,128)(2,1)} %param.20) | copy-start | bytes 1572868
where the time goes:
time: 682 us; the launch traced here: 681 us
  blocking collectives  257 us (38%)
  waiting for transfers between devices  195 us (29%)
  starting transfers between devices  121 us (18%)
  matrix products  43.8 us (6%)
  local copies, waits for them, and re-layouts  40.4 us (6%)
  other arithmetic  22.8 us (3%)
    ppermute x9, waiting for transfers between devices, from_behind(): return lax.ppermute(array, axis, pairs)  180 us
    psum x2, blocking collectives, group_norm(): mean = lax.psum(local_sum, ('tm', 'rows')) / count  130 us
    psum x2, blocking collectives, group_norm(): lax.psum(jnp.sum(centered * centered, axis=(0, 1, 2, 4)), ('tm', 'rows'))  127 us
    ppermute x9, starting transfers between devices, from_behind(): return lax.ppermute(array, axis, pairs)  115 us
    unnamed x65, local copies, waits for them, and re-layouts  17.3 us
    dot_general x9, matrix products, conv_taps(): jnp.dot(stacked.reshape(-1, 3 * chans), weight[step_t, step_h].reshape(3...  15.9 us
  transfers between devices with their start and end apart: 11, of which 7 were waited for; matrix products, arithmetic and copies ran while one was open for 4% of the time, Pallas kernels for 0%

commit v1 on v0

--- a/solution.py
+++ b/solution.py
@@ -38,7 +38,9 @@
     local_sum = jnp.sum(grouped, axis=(0, 1, 2, 4))
     mean = lax.psum(local_sum, ("tm", "rows")) / count
     centered = grouped - mean[:, None]
-    spread = lax.psum(jnp.sum(centered * centered, axis=(0, 1, 2, 4)), ("tm", "rows")) / count
+    spread = (
+        lax.psum(lax.psum(jnp.sum(centered * centered, axis=(0, 1, 2, 4)), "tm"), "rows") / count
+    )
     normed = centered * lax.rsqrt(spread + EPS)[:, None]
     return normed.reshape(values.shape) * gain + shift
 

time: 682 us -> 849 us (1.24)
  blocking collectives: 257 us -> 464 us
  starting transfers between devices: 121 us -> 85.5 us
    psum x2 -> x4, blocking collectives: 127 us -> 321 us  [the longest x2 316 us: group_norm(): lax.psum(lax.psum(jnp.sum(centered * centered, axis=(0, 1, 2, 4)), 'tm'),...]
    ppermute x9, starting transfers between devices: 115 us -> 79.2 us  [from_behind(): return lax.ppermute(array, axis, pairs)]
    psum x2, blocking collectives: 130 us -> 142 us  [group_norm(): mean = lax.psum(local_sum, ('tm', 'rows')) / count]
  transfers between devices with their start and end apart: 11 -> 11, of which waited for: 7 -> 8; matrix products, arithmetic and copies ran while one was open for 4% -> 3% of each run, Pallas kernels for 0% -> 0%
where the time goes in v1:
time: 849 us; the launch traced here: 848 us
  blocking collectives  464 us (55%)
  waiting for transfers between devices  191 us (22%)
  starting transfers between devices  85.5 us (10%)
  matrix products  43.9 us (5%)
  local copies, waits for them, and re-layouts  40.4 us (5%)
  other arithmetic  22.8 us (3%)
    psum x2, blocking collectives, group_norm(): lax.psum(lax.psum(jnp.sum(centered * centered, axis=(0, 1, 2, 4)), 'tm'),...  316 us
    ppermute x9, waiting for transfers between devices, from_behind(): return lax.ppermute(array, axis, pairs)  173 us
    psum x2, blocking collectives, group_norm(): mean = lax.psum(local_sum, ('tm', 'rows')) / count  142 us
    ppermute x9, starting transfers between devices, from_behind(): return lax.ppermute(array, axis, pairs)  79.2 us
    unnamed x65, local copies, waits for them, and re-layouts  17.3 us
  transfers between devices with their start and end apart: 11, of which 8 were waited for; matrix products, arithmetic and copies ran while one was open for 3% of the time, Pallas kernels for 0%

profile of v1, /device:TPU:54, one launch (start us, length us, event | category | flops | bytes accessed | tf_op | source)
XLA Modules:
  0.0 848.1 jit_solution(14524751550684099938)
XLA Ops:
  1.7 63.7 %psum.42 = f32[32]{0:T(128)S(1)} all-reduce(f32[32]{0:T(128)S(1)} %reduce_sum.59), channel_id=1, replica_groups=mesh['tm'=2,'rows'=64] {'tm','rows'}, use_global_device_ids=true, to_apply=%region_2.0 | all-reduce | flops 32 | bytes 256 | tf_op jit(solution)/shard_map/psum | solution.py:39
  67.2 2.5 psum.43
  69.7 150.9 %psum.44 = f32[32]{0:T(128)S(1)} all-reduce(f32[32]{0:T(128)S(1)} %psum.43), channel_id=1, replica_groups=mesh['tm'=2,'rows'=64] {'rows'}, use_global_device_ids=true, to_apply=%region_6.7 | all-reduce | flops 32 | bytes 256 | tf_op jit(solution)/shard_map/psum | solution.py:42
  220.8 1.9 fusion.31
  224.1 2.1 collective-permute-done
  226.5 4.2 collective-permute-start.1
  230.7 2.1 collective-permute-start.2
  232.8 9.2 %fusion.44 = (bf16[1,1,3,512,512]{4,3,2,1,0:T(8,128)(2,1)S(1)}, bf16[1,1,3,512,512]{4,3,2,1,0:T(8,128)(2,1)}, bf16[1,1,3,512,512]{4,3,2,1,0:T(8,128)(2,1)}, bf16...) fusion(bf16[3,3,3,512,512]{4,3,2,1,0:T(8,128)(2,1)} %param.15), kind=kLoop, calls=%fused_computation.89 | loop fusion | bytes 28311552 | tf_op jit(solution)/shard_map/slice | solution.py:59
  242.0 10.4 %collective-permute-done.1 = bf16[4,1,240,512]{3,2,1,0:T(8,128)(2,1)S(1)} collective-permute-done((bf16[4,1,240,512]{3,2,1,0:T(8,128)(2,1)S(1)}, bf16[4,1,240,512]{3,2,1,0:T(8,128)(2,1)S(1)}, u32[]{:S(2)}, u32[]{:S(2)}) %collective-permute-start.1) | collective-permute-done | bytes 983072 | tf_op jit(solution)/shard_map/ppermute | solution.py:26
  252.4 8.2 collective-permute-done.2
  260.6 2.1 select_maximum_fusion
  262.7 6.3 fusion.45
  273.3 1.7 fusion.48
  275.1 1.7 fusion.50
  278.5 1.7 fusion.51
  280.2 1.7 fusion.53
  283.3 1.7 fusion.54
  286.4 1.7 fusion.49
  288.2 1.7 fusion.52
  289.8 1.7 fusion.55
  291.6 2.5 add_add_fusion
  294.7 78.8 %psum.45 = f32[32]{0:T(128)S(1)} all-reduce(f32[32]{0:T(128)S(1)} %reduce_sum.81), channel_id=1, replica_groups=mesh['tm'=2,'rows'=64] {'tm','rows'}, use_global_device_ids=true, to_apply=%region_9.10 | all-reduce | flops 32 | bytes 256 | tf_op jit(solution)/shard_map/psum | solution.py:39
  374.2 2.5 psum.46
  376.6 165.2 %psum.47 = f32[32]{0:T(128)S(1)} all-reduce(f32[32]{0:T(128)S(1)} %psum.46), channel_id=1, replica_groups=mesh['tm'=2,'rows'=64] {'rows'}, use_global_device_ids=true, to_apply=%region_13.14 | all-reduce | flops 32 | bytes 256 | tf_op jit(solution)/shard_map/psum | solution.py:42
  543.1 1.7 convolution_convert_fusion
  546.3 2.3 collective-permute-start.3
  548.7 1.9 collective-permute-start.4
  550.6 5.7 collective-permute-start.5
  556.3 1.9 collective-permute-start.6
  558.2 3.9 collective-permute-start.7
  562.2 32.8 %collective-permute-done.3 = bf16[2,2,2,240,512]{4,3,2,1,0:T(8,128)(2,1)} collective-permute-done((bf16[2,2,2,240,512]{4,3,2,1,0:T(8,128)(2,1)}, bf16[2,2,2,240,512]{4,3,2,1,0:T(8,128)(2,1)}, u32[]{:S(2)}, u32[]{:S(2)}) %collective-permute-start.3) | collective-permute-done | bytes 1966112 | tf_op jit(solution)/shard_map/ppermute | solution.py:15
  594.9 1.9 collective-permute-start.8
  596.8 31.3 %collective-permute-done.4 = bf16[2,2,2,240,512]{4,3,2,1,0:T(8,128)(2,1)} collective-permute-done((bf16[2,2,2,240,512]{4,3,2,1,0:T(8,128)(2,1)}, bf16[2,2,2,240,512]{4,3,2,1,0:T(8,128)(2,1)}, u32[]{:S(2)}, u32[]{:S(2)}) %collective-permute-start.4) | collective-permute-done | bytes 1966112 | tf_op jit(solution)/shard_map/ppermute | solution.py:15
  628.1 58.3 %collective-permute-start.9 = (bf16[2,2,2,240,512]{4,3,2,1,0:T(8,128)(2,1)}, bf16[2,2,2,240,512]{4,3,2,1,0:T(8,128)(2,1)}, u32[]{:S(2)}, u32[]{:S(2)}) collective-permute-start(bf16[2,2,2,240,512]{4,3,2,1,0:T(8,128)(2,1)} %pad_maximum_fusion.10), channel_id=1, source_target_pairs={{3,0},{4,1},{5,2},{6,3},{7,4},{8,5},{9,6},{10,7},{11,8},{12,9},{13... | collective-permute-start | bytes 5898248 | tf_op jit(solution)/shard_map/ppermute | solution.py:15
  686.4 1.9 collective-permute-start.10
  688.5 2.8 convolution_convert_fusion.2
  693.0 1.7 constant_dynamic-update-slice_fusion.7
  694.7 1.7 constant_dynamic-update-slice_fusion.6
  696.4 1.7 constant_dynamic-update-slice_fusion.5
  698.2 1.7 constant_dynamic-update-slice_fusion.3
  699.9 2.9 collective-permute-done.8
  704.4 25.6 %collective-permute-done.9 = bf16[2,2,2,240,512]{4,3,2,1,0:T(8,128)(2,1)} collective-permute-done((bf16[2,2,2,240,512]{4,3,2,1,0:T(8,128)(2,1)}, bf16[2,2,2,240,512]{4,3,2,1,0:T(8,128)(2,1)}, u32[]{:S(2)}, u32[]{:S(2)}) %collective-permute-start.9) | collective-permute-done | bytes 1966112 | tf_op jit(solution)/shard_map/ppermute | solution.py:15
  731.6 78.1 %collective-permute-done.10 = bf16[2,2,2,240,512]{4,3,2,1,0:T(8,128)(2,1)} collective-permute-done((bf16[2,2,2,240,512]{4,3,2,1,0:T(8,128)(2,1)}, bf16[2,2,2,240,512]{4,3,2,1,0:T(8,128)(2,1)}, u32[]{:S(2)}, u32[]{:S(2)}) %collective-permute-start.10) | collective-permute-done | bytes 1966112 | tf_op jit(solution)/shard_map/ppermute | solution.py:15
  809.7 1.7 constant_dynamic-update-slice_fusion
  811.4 4.3 fusion.43
  815.7 10.1 %fusion = (f32[2,480]{1,0:T(2,128)S(1)}, f32[2,480,4320]{2,1,0:T(8,128)}) fusion(pred[4320]{0:T(1024)(128)(4,1)S(1)} %broadcast_in_dim.35, bf16[2,480,512]{2,1,0:T(8,128)(2,1)} %bitcast.89, bf16[2,4320,512]{2,1,0:T(8,128)(2,1)S(1)} %bitcast.63), kind=kOutput, calls=%fused_computation.2 | convolution fusion | flops 4259173376 | bytes 26427360 | tf_op jit(solution)/shard_map/fqc,fkc->fqk/dot_general | solution.py:119
  825.9 9.5 %fusion.1 = f32[2,480]{1,0:T(2,128)S(1)} fusion(f32[2,480,4320]{2,1,0:T(8,128)} %get-tuple-element.50, f32[2,480]{1,0:T(2,128)S(1)} %get-tuple-element.49, pred[4320]{0:T(1024)(128)(4,1)S(1)} %broadcast_in_dim.35), kind=kLoop, calls=%fused_computation.3 | loop fusion | flops 16587840 | bytes 16600800 | tf_op jit(solution)/shard_map/reduce_sum | solution.py:123
  835.4 11.1 %divide_convert_fusion = bf16[2,480,512]{2,1,0:T(8,128)(2,1)S(1)} fusion(bf16[2,4320,512]{2,1,0:T(8,128)(2,1)} %bitcast.62, f32[2,480,4320]{2,1,0:T(8,128)} %get-tuple-element.50, f32[2,480]{1,0:T(2,128)S(1)} %get-tuple-element.49, pred[4320]{0:T(1024)(128)(4,1)S(1)} %broadcast_in_dim.35, f32[2,480]{1,0:T(2,128)S(1)} %fusion.1), kind=kOutput, calls=%fused_computation.62 | convolution fusion | flops 4264304640 | bytes 26431200 | tf_op jit(solution)/shard_map/fqk,fkc->fqc/dot_general | solution.py:124
  (107 shorter events, 25.3 us)
Async XLA Ops:
  0.0 542.4 %copy-start = (bf16[512,512]{1,0:T(8,128)(2,1)S(1)}, bf16[512,512]{1,0:T(8,128)(2,1)}, u32[]{:S(2)}) copy-start(bf16[512,512]{1,0:T(8,128)(2,1)} %param.20) | copy-start | bytes 1572868
  222.7 3.5 collective-permute-start
  226.5 25.9 %collective-permute-start.1 = (bf16[4,1,240,512]{3,2,1,0:T(8,128)(2,1)S(1)}, bf16[4,1,240,512]{3,2,1,0:T(8,128)(2,1)S(1)}, u32[]{:S(2)}, u32[]{:S(2)}) collective-permute-start(bf16[4,1,240,512]{3,2,1,0:T(8,128)(2,1)S(1)} %get-tuple-element.44), channel_id=1, source_target_pairs={{0,1},{1,2},{2,3},{3,4},{4,5},{5,6},{6,7},{7,8},{8,9},{9,10},{10,1... | collective-permute-start | bytes 2949128 | tf_op jit(solution)/shard_map/ppermute | solution.py:26
  230.7 29.9 %collective-permute-start.2 = (bf16[4,1,240,512]{3,2,1,0:T(8,128)(2,1)S(1)}, bf16[4,1,240,512]{3,2,1,0:T(8,128)(2,1)S(1)}, u32[]{:S(2)}, u32[]{:S(2)}) collective-permute-start(bf16[4,1,240,512]{3,2,1,0:T(8,128)(2,1)S(1)} %get-tuple-element.45), channel_id=1, source_target_pairs={{1,0},{2,1},{3,2},{4,3},{5,4},{6,5},{7,6},{8,7},{9,8},{10,9},{11,1... | collective-permute-start | bytes 2949128 | tf_op jit(solution)/shard_map/ppermute | solution.py:28
  269.8 1.2 copy-start.10
  269.8 1.5 copy-start.11
  269.8 1.8 copy-start.12
  269.9 2.1 copy-start.13
  271.9 1.4 copy-start.21
  273.3 1.7 copy-start.20
  275.0 1.7 copy-start.6
  275.0 1.7 copy-start.7
  275.0 1.8 copy-start.8
  275.1 2.1 copy-start.9
  277.1 1.4 copy-start.19
  278.5 1.7 copy-start.18
  280.2 1.7 copy-start.5
  281.9 1.4 copy-start.17
  285.0 1.4 copy-start.16
  286.4 1.7 copy-start.15
  288.1 1.7 copy-start.14
  291.5 2.5 copy-start.2
  291.5 2.5 copy-start.24
  294.0 248.0 %copy-start.25 = (f32[512]{0:T(512)S(1)}, f32[512]{0:T(512)}, u32[]{:S(2)}) copy-start(f32[512]{0:T(512)} %param.18) | copy-start | bytes 6148
  294.0 248.0 %copy-start.26 = (f32[512]{0:T(512)S(1)}, f32[512]{0:T(512)}, u32[]{:S(2)}) copy-start(f32[512]{0:T(512)} %param.17) | copy-start | bytes 6148
  294.5 248.6 %copy-start.3 = (bf16[2,2,240,512]{3,2,1,0:T(8,128)(2,1)}, bf16[2,2,240,512]{3,2,1,0:T(8,128)(2,1)S(1)}, u32[]{:S(2)}) copy-start(bf16[2,2,240,512]{3,2,1,0:T(8,128)(2,1)S(1)} %get-tuple-element.6) | copy-start | bytes 2949124
  542.4 2.4 copy-start.22
  544.8 143.7 %copy-start.23 = (bf16[2,2,240,512]{3,2,1,0:T(8,128)(2,1)S(1)}, bf16[2,2,240,512]{3,2,1,0:T(8,128)(2,1)}, u32[]{:S(2)}) copy-start(bf16[2,2,240,512]{3,2,1,0:T(8,128)(2,1)} %copy-done.22) | copy-start | bytes 2949124
  546.3 48.6 %collective-permute-start.3 = (bf16[2,2,2,240,512]{4,3,2,1,0:T(8,128)(2,1)}, bf16[2,2,2,240,512]{4,3,2,1,0:T(8,128)(2,1)}, u32[]{:S(2)}, u32[]{:S(2)}) collective-permute-start(bf16[2,2,2,240,512]{4,3,2,1,0:T(8,128)(2,1)} %pad_maximum_fusion.10), channel_id=1, source_target_pairs={{0,4},{1,5},{2,6},{3,7},{4,8},{5,9},{6,10},{7,11},{8,12},{9,13},{1... | collective-permute-start | bytes 5898248 | tf_op jit(solution)/shard_map/ppermute | solution.py:15
  548.7 79.5 %collective-permute-start.4 = (bf16[2,2,2,240,512]{4,3,2,1,0:T(8,128)(2,1)}, bf16[2,2,2,240,512]{4,3,2,1,0:T(8,128)(2,1)}, u32[]{:S(2)}, u32[]{:S(2)}) collective-permute-start(bf16[2,2,2,240,512]{4,3,2,1,0:T(8,128)(2,1)} %pad_maximum_fusion.10), channel_id=1, source_target_pairs={{0,3},{1,4},{2,5},{3,6},{4,7},{5,8},{6,9},{7,10},{8,11},{9,12},{10... | collective-permute-start | bytes 5898248 | tf_op jit(solution)/shard_map/ppermute | solution.py:15
  550.6 135.8 %collective-permute-start.5 = (bf16[2,2,2,240,512]{4,3,2,1,0:T(8,128)(2,1)}, bf16[2,2,2,240,512]{4,3,2,1,0:T(8,128)(2,1)}, u32[]{:S(2)}, u32[]{:S(2)}) collective-permute-start(bf16[2,2,2,240,512]{4,3,2,1,0:T(8,128)(2,1)} %pad_maximum_fusion.10), channel_id=1, source_target_pairs={{0,2},{1,3},{2,4},{3,5},{4,6},{5,7},{6,8},{7,9},{8,10},{9,11},{10,... | collective-permute-start | bytes 5898248 | tf_op jit(solution)/shard_map/ppermute | solution.py:15
  556.3 140.1 %collective-permute-start.6 = (bf16[2,2,2,240,512]{4,3,2,1,0:T(8,128)(2,1)}, bf16[2,2,2,240,512]{4,3,2,1,0:T(8,128)(2,1)}, u32[]{:S(2)}, u32[]{:S(2)}) collective-permute-start(bf16[2,2,2,240,512]{4,3,2,1,0:T(8,128)(2,1)} %pad_maximum_fusion.10), channel_id=1, source_target_pairs={{0,1},{1,2},{2,3},{3,4},{4,5},{5,6},{6,7},{7,8},{8,9},{9,10},{10,1... | collective-permute-start | bytes 5898248 | tf_op jit(solution)/shard_map/ppermute | solution.py:15
  558.2 139.9 %collective-permute-start.7 = (bf16[2,2,2,240,512]{4,3,2,1,0:T(8,128)(2,1)}, bf16[2,2,2,240,512]{4,3,2,1,0:T(8,128)(2,1)}, u32[]{:S(2)}, u32[]{:S(2)}) collective-permute-start(bf16[2,2,2,240,512]{4,3,2,1,0:T(8,128)(2,1)} %pad_maximum_fusion.10), channel_id=1, source_target_pairs={{1,0},{2,1},{3,2},{4,3},{5,4},{6,5},{7,6},{8,7},{9,8},{10,9},{11,1... | collective-permute-start | bytes 5898248 | tf_op jit(solution)/shard_map/ppermute | solution.py:15
  594.9 107.8 %collective-permute-start.8 = (bf16[2,2,2,240,512]{4,3,2,1,0:T(8,128)(2,1)}, bf16[2,2,2,240,512]{4,3,2,1,0:T(8,128)(2,1)}, u32[]{:S(2)}, u32[]{:S(2)}) collective-permute-start(bf16[2,2,2,240,512]{4,3,2,1,0:T(8,128)(2,1)} %pad_maximum_fusion.10), channel_id=1, source_target_pairs={{2,0},{3,1},{4,2},{5,3},{6,4},{7,5},{8,6},{9,7},{10,8},{11,9},{12,... | collective-permute-start | bytes 5898248 | tf_op jit(solution)/shard_map/ppermute | solution.py:15
  628.1 101.8 %collective-permute-start.9 = (bf16[2,2,2,240,512]{4,3,2,1,0:T(8,128)(2,1)}, bf16[2,2,2,240,512]{4,3,2,1,0:T(8,128)(2,1)}, u32[]{:S(2)}, u32[]{:S(2)}) collective-permute-start(bf16[2,2,2,240,512]{4,3,2,1,0:T(8,128)(2,1)} %pad_maximum_fusion.10), channel_id=1, source_target_pairs={{3,0},{4,1},{5,2},{6,3},{7,4},{8,5},{9,6},{10,7},{11,8},{12,9},{13... | collective-permute-start | bytes 5898248 | tf_op jit(solution)/shard_map/ppermute | solution.py:15
  686.4 123.3 %collective-permute-start.10 = (bf16[2,2,2,240,512]{4,3,2,1,0:T(8,128)(2,1)}, bf16[2,2,2,240,512]{4,3,2,1,0:T(8,128)(2,1)}, u32[]{:S(2)}, u32[]{:S(2)}) collective-permute-start(bf16[2,2,2,240,512]{4,3,2,1,0:T(8,128)(2,1)} %pad_maximum_fusion.10), channel_id=1, source_target_pairs={{4,0},{5,1},{6,2},{7,3},{8,4},{9,5},{10,6},{11,7},{12,8},{13,9},{1... | collective-permute-start | bytes 5898248 | tf_op jit(solution)/shard_map/ppermute | solution.py:15
  835.3 11.1 %copy-start.4 = (bf16[2,2,240,512]{3,2,1,0:T(8,128)(2,1)S(1)}, bf16[2,2,240,512]{3,2,1,0:T(8,128)(2,1)}, u32[]{:S(2)}) copy-start(bf16[2,2,240,512]{3,2,1,0:T(8,128)(2,1)} %copy-done.3) | copy-start | bytes 2949124
  835.3 11.1 %copy-start.27 = (bf16[512,512]{1,0:T(8,128)(2,1)S(1)}, bf16[512,512]{1,0:T(8,128)(2,1)}, u32[]{:S(2)}) copy-start(bf16[512,512]{1,0:T(8,128)(2,1)} %param.22) | copy-start | bytes 1572868
  835.3 11.1 %copy-start.28 = (f32[512]{0:T(512)S(1)}, f32[512]{0:T(512)}, u32[]{:S(2)}) copy-start(f32[512]{0:T(512)} %param.23) | copy-start | bytes 6148
  835.3 12.7 %copy-start.1 = (bf16[512,512]{1,0:T(8,128)(2,1)S(1)}, bf16[512,512]{1,0:T(8,128)(2,1)}, u32[]{:S(2)}) copy-start(bf16[512,512]{1,0:T(8,128)(2,1)} %param.20) | copy-start | bytes 1572868
